TPU v7x, 32 devices: a whole 2x2x4 slice. The times are simulated.
32 devices in a mesh: ev: 8 (over y, x, core), st: 4 (over z).
Axes of the slice: x: 2, y: 2, z: 4, core: 2. Of those that a mesh axis runs over, the one named last changes fastest.
Arguments:
- amplitudes: bfloat16 [131072, 2048], P(('ev', 'st')), may hold values from -6 to 6
- event_mass: float32 [131072], P(('ev', 'st')), may hold values from 0.8 to 2.5
- data_rows: int32 [32], P(('ev', 'st')), may hold values from 256 to 2560, as said below
- wave_shape: int32 [1024], replicated, may hold values from 0 to 31
- pole_mass: float32 [32], replicated, may hold values from 1 to 2.3
- pole_width: float32 [32], replicated, may hold values from 0.1 to 0.5
- coefficients: float32 [128, 2048], replicated, may hold values from -6 to 6
- background: float32 [128], replicated, may hold values from 0.2 to 2
Outputs:
- gradient: float32 [128, 2048], P('st')
- likelihood: float32 [128], P('st')
Inputs may be any that keep to these rules, and one draw needn't show every extreme that they name: `data_rows`: each device holds its data events first; the share of data events differs strongly from device to device.
All inputs are finite; a program needn't handle non-finite values.
Results may differ from a plain program's by a relative error of at most 0.0032.
Values sent between devices are 32-bit elements; how exact they have to be, the bound alone decides.
A program may use at most 64 MiB of HBM per device.

v0:
```python
import jax
import jax.numpy as jnp
from jax import lax
from jax.sharding import PartitionSpec as P

BLOCK = 512


def fold_parts(block):
    half_s = block.shape[0] // 2
    half_w = block.shape[1] // 2
    real_part = block[:half_s, :half_w] + block[half_s:, half_w:]
    imag_part = block[half_s:, :half_w] - block[:half_s, half_w:]
    return jnp.concatenate([real_part, imag_part], 1)


def reduce_all(grads, sums):
    whole = lax.psum((grads, sums), "ev")
    return (
        lax.psum_scatter(whole[0], "st", scatter_dimension=1, tiled=True),
        lax.psum_scatter(whole[1], "st", scatter_dimension=1, tiled=True),
    )


def shards(
    amplitudes, event_mass, data_rows, wave_shape, pole_mass, pole_width, coefficients, background
):
    rows = amplitudes.shape[0]
    waves = amplitudes.shape[1] // 2
    starts = coefficients.shape[0]
    shapes = pole_mass.shape[0]
    scale = waves ** (-0.5)
    n_data = lax.psum(data_rows.astype(jnp.float32)[0], ("ev", "st"))
    n_sim = rows * lax.axis_size("ev") * lax.axis_size("st") - n_data
    coef = coefficients.astype(jnp.bfloat16)
    coef_real = coef[:, :waves].T
    coef_imag = coef[:, waves:].T
    mixing = jnp.concatenate(
        [jnp.concatenate([coef_real, coef_imag], 1), jnp.concatenate([-coef_imag, coef_real], 1)], 0
    )
    selector = wave_shape[None, :] == jnp.arange(shapes, dtype=jnp.int32)[:, None]
    peak = pole_mass * pole_width
    square = pole_mass * pole_mass
    wave_peak = jnp.sum(jnp.where(selector, peak[:, None], 0.0), 0)
    wave_peak2 = jnp.sum(jnp.where(selector, (peak * peak)[:, None], 0.0), 0)
    wave_square = jnp.sum(jnp.where(selector, square[:, None], 0.0), 0)
    limit = data_rows[0]

    def block_step(index, carry):
        grads, log_sum, sim_sum = carry
        first = index * BLOCK
        piece = lax.dynamic_slice_in_dim(amplitudes, first, BLOCK, 0)
        mass = lax.dynamic_slice_in_dim(event_mass, first, BLOCK, 0)
        offset = wave_square[None, :] - (mass * mass)[:, None]
        denom = offset * offset + wave_peak2[None, :]
        wide_real = wave_peak[None, :] * offset / denom
        wide_imag = wave_peak2[None, :] / denom
        amp_real = piece[:, :waves].astype(jnp.float32)
        amp_imag = piece[:, waves:].astype(jnp.float32)
        dressed = jnp.concatenate(
            [
                amp_real * wide_real - amp_imag * wide_imag,
                amp_real * wide_imag + amp_imag * wide_real,
            ],
            1,
        ).astype(jnp.bfloat16)
        value = jnp.dot(dressed, mixing, preferred_element_type=jnp.float32) * scale
        val_real = value[:, :starts]
        val_imag = value[:, starts:]
        intensity = val_real * val_real + val_imag * val_imag + background[None, :]
        is_data = (first + jnp.arange(BLOCK, dtype=jnp.int32) < limit)[:, None]
        log_sum = log_sum + jnp.sum(jnp.where(is_data, jnp.log(intensity), 0.0), 0)
        sim_sum = sim_sum + jnp.sum(jnp.where(is_data, 0.0, intensity), 0)
        factor = jnp.where(is_data, -1.0 / intensity, 1.0)
        weighted = (2.0 * jnp.concatenate([factor, factor], 1) * value).astype(jnp.bfloat16)
        nothing = jnp.zeros_like(weighted)
        split = jnp.concatenate(
            [jnp.where(is_data, weighted, nothing), jnp.where(is_data, nothing, weighted)], 1
        )
        grads = grads + lax.dot_general(
            split, dressed, (((0,), (0,)), ((), ())), preferred_element_type=jnp.float32
        )
        return (grads, log_sum, sim_sum)

    start = (
        jnp.zeros((4 * starts, 2 * waves), jnp.float32),
        jnp.zeros((starts,), jnp.float32),
        jnp.zeros((starts,), jnp.float32),
    )
    grads, log_sum, sim_sum = lax.fori_loop(0, rows // BLOCK, block_step, start)
    data_part = fold_parts(grads[: 2 * starts]) * scale
    sim_part = fold_parts(grads[2 * starts :]) * scale
    local_grad = jnp.stack([data_part, sim_part], 0)
    local_sums = jnp.stack([log_sum, sim_sum], 0)
    total_grad, total_sums = reduce_all(local_grad, local_sums)
    gradient = waves * (total_grad[0] / n_data + total_grad[1] / n_sim)
    likelihood = -total_sums[0] / n_data + total_sums[1] / n_sim
    return (gradient, likelihood)


def solution(mesh):
    return jax.shard_map(
        shards,
        mesh=mesh,
        in_specs=(P(("ev", "st"), None), P(("ev", "st")), P(("ev", "st")), P(), P(), P(), P(), P()),
        out_specs=(P("st", None), P("st")),
        check_vma=False,
    )
```

profile of v0, /device:TPU:0, one launch (start us, length us, event | category | flops | bytes accessed | tf_op | source)
XLA Modules:
  0.0 230.2 jit_solution(12513770014983048937)
XLA Ops:
  7.2 1.5 copy.12
  9.6 83.3 %while.18 = (s32[]{:T(128)}, f32[512,2048]{1,0:T(8,128)}, f32[128]{0:T(128)S(1)}, f32[128]{0:T(128)S(1)}, s32[]{:T(128)}, /*index=5*/bf16[4096,2048]{1,0:T(8,128...) while((s32[]{:T(128)}, f32[512,2048]{1,0:T(8,128)}, ...), condition=%wide.region_6.7_spmd.clone, body=%wide.region_3.6_spmd.clone.sunk | while | flops 1632110336 | bytes 55075632 | solution.py:90
  10.3 0.8 dynamic-slice_multiply_fusion.2
  11.0 3.0 %fusion.35 = (bf16[512,1024]{1,0:T(8,128)(2,1)S(1)}, bf16[512,1024]{1,0:T(8,128)(2,1)S(1)}) fusion(f32[1024]{0:T(1024)S(1)} %get-tuple-element.426, f32[512]{0:T(512)S(1)} %dynamic-slice_multiply_fusion.2, f32[1024]{0:T(1024)S(1)} %get-tuple-element.424, f32[1024]{0:T(1024)S(1)} %get-tuple-element.423, bf16[4096,2048]{1,0:T(8,128)(2,1)} %get-tuple-element.422, ...), kind=kLoop, calls=%fused_computation.8.clone.1 | loop fusion | flops 8388608 | bytes 4208648 | tf_op jit(solution)/shard_map/convert
  15.2 1.0 copy-done
  16.2 1.9 select_add_fusion.2
  18.1 1.9 copy-done.1
  20.7 0.8 dynamic-slice_multiply_fusion.2
  21.4 3.0 %fusion.35 = (bf16[512,1024]{1,0:T(8,128)(2,1)S(1)}, bf16[512,1024]{1,0:T(8,128)(2,1)S(1)}) fusion(f32[1024]{0:T(1024)S(1)} %get-tuple-element.426, f32[512]{0:T(512)S(1)} %dynamic-slice_multiply_fusion.2, f32[1024]{0:T(1024)S(1)} %get-tuple-element.424, f32[1024]{0:T(1024)S(1)} %get-tuple-element.423, bf16[4096,2048]{1,0:T(8,128)(2,1)} %get-tuple-element.422, ...), kind=kLoop, calls=%fused_computation.8.clone.1 | loop fusion | flops 8388608 | bytes 4208648 | tf_op jit(solution)/shard_map/convert
  25.7 1.0 copy-done
  26.6 1.9 select_add_fusion.2
  28.5 1.9 copy-done.1
  31.1 0.8 dynamic-slice_multiply_fusion.2
  31.9 3.0 %fusion.35 = (bf16[512,1024]{1,0:T(8,128)(2,1)S(1)}, bf16[512,1024]{1,0:T(8,128)(2,1)S(1)}) fusion(f32[1024]{0:T(1024)S(1)} %get-tuple-element.426, f32[512]{0:T(512)S(1)} %dynamic-slice_multiply_fusion.2, f32[1024]{0:T(1024)S(1)} %get-tuple-element.424, f32[1024]{0:T(1024)S(1)} %get-tuple-element.423, bf16[4096,2048]{1,0:T(8,128)(2,1)} %get-tuple-element.422, ...), kind=kLoop, calls=%fused_computation.8.clone.1 | loop fusion | flops 8388608 | bytes 4208648 | tf_op jit(solution)/shard_map/convert
  36.1 1.0 copy-done
  37.0 1.9 select_add_fusion.2
  38.9 1.9 copy-done.1
  41.5 0.8 dynamic-slice_multiply_fusion.2
  42.3 3.0 %fusion.35 = (bf16[512,1024]{1,0:T(8,128)(2,1)S(1)}, bf16[512,1024]{1,0:T(8,128)(2,1)S(1)}) fusion(f32[1024]{0:T(1024)S(1)} %get-tuple-element.426, f32[512]{0:T(512)S(1)} %dynamic-slice_multiply_fusion.2, f32[1024]{0:T(1024)S(1)} %get-tuple-element.424, f32[1024]{0:T(1024)S(1)} %get-tuple-element.423, bf16[4096,2048]{1,0:T(8,128)(2,1)} %get-tuple-element.422, ...), kind=kLoop, calls=%fused_computation.8.clone.1 | loop fusion | flops 8388608 | bytes 4208648 | tf_op jit(solution)/shard_map/convert
  46.5 1.0 copy-done
  47.5 1.9 select_add_fusion.2
  49.3 1.9 copy-done.1
  51.9 0.8 dynamic-slice_multiply_fusion.2
  52.7 3.0 %fusion.35 = (bf16[512,1024]{1,0:T(8,128)(2,1)S(1)}, bf16[512,1024]{1,0:T(8,128)(2,1)S(1)}) fusion(f32[1024]{0:T(1024)S(1)} %get-tuple-element.426, f32[512]{0:T(512)S(1)} %dynamic-slice_multiply_fusion.2, f32[1024]{0:T(1024)S(1)} %get-tuple-element.424, f32[1024]{0:T(1024)S(1)} %get-tuple-element.423, bf16[4096,2048]{1,0:T(8,128)(2,1)} %get-tuple-element.422, ...), kind=kLoop, calls=%fused_computation.8.clone.1 | loop fusion | flops 8388608 | bytes 4208648 | tf_op jit(solution)/shard_map/convert
  56.9 1.0 copy-done
  57.9 1.9 select_add_fusion.2
  59.8 1.9 copy-done.1
  63.1 3.0 %fusion.35 = (bf16[512,1024]{1,0:T(8,128)(2,1)S(1)}, bf16[512,1024]{1,0:T(8,128)(2,1)S(1)}) fusion(f32[1024]{0:T(1024)S(1)} %get-tuple-element.426, f32[512]{0:T(512)S(1)} %dynamic-slice_multiply_fusion.2, f32[1024]{0:T(1024)S(1)} %get-tuple-element.424, f32[1024]{0:T(1024)S(1)} %get-tuple-element.423, bf16[4096,2048]{1,0:T(8,128)(2,1)} %get-tuple-element.422, ...), kind=kLoop, calls=%fused_computation.8.clone.1 | loop fusion | flops 8388608 | bytes 4208648 | tf_op jit(solution)/shard_map/convert
  67.3 1.0 copy-done
  68.3 1.9 select_add_fusion.2
  70.2 1.9 copy-done.1
  73.5 3.0 %fusion.35 = (bf16[512,1024]{1,0:T(8,128)(2,1)S(1)}, bf16[512,1024]{1,0:T(8,128)(2,1)S(1)}) fusion(f32[1024]{0:T(1024)S(1)} %get-tuple-element.426, f32[512]{0:T(512)S(1)} %dynamic-slice_multiply_fusion.2, f32[1024]{0:T(1024)S(1)} %get-tuple-element.424, f32[1024]{0:T(1024)S(1)} %get-tuple-element.423, bf16[4096,2048]{1,0:T(8,128)(2,1)} %get-tuple-element.422, ...), kind=kLoop, calls=%fused_computation.8.clone.1 | loop fusion | flops 8388608 | bytes 4208648 | tf_op jit(solution)/shard_map/convert
  77.7 1.0 copy-done
  78.7 1.9 select_add_fusion.2
  80.6 1.9 copy-done.1
  83.9 3.0 %fusion.35 = (bf16[512,1024]{1,0:T(8,128)(2,1)S(1)}, bf16[512,1024]{1,0:T(8,128)(2,1)S(1)}) fusion(f32[1024]{0:T(1024)S(1)} %get-tuple-element.426, f32[512]{0:T(512)S(1)} %dynamic-slice_multiply_fusion.2, f32[1024]{0:T(1024)S(1)} %get-tuple-element.424, f32[1024]{0:T(1024)S(1)} %get-tuple-element.423, bf16[4096,2048]{1,0:T(8,128)(2,1)} %get-tuple-element.422, ...), kind=kLoop, calls=%fused_computation.8.clone.1 | loop fusion | flops 8388608 | bytes 4208648 | tf_op jit(solution)/shard_map/convert
  88.1 1.0 copy-done
  89.1 1.9 select_add_fusion.2
  91.0 1.9 copy-done.1
  92.9 2.5 %add_bitcast_fusion.1 = (f32[1,128,1024]{2,1,0:T(8,128)S(1)}, f32[1,128,1024]{2,1,0:T(8,128)S(1)}, f32[1,128,1024]{2,1,0:T(8,128)S(1)}, f32[1,128,1024]{2,1,0:T(8,128)S(1)}) fusion(f32[512,2048]{1,0:T(8,128)} %get-tuple-element.203), kind=kLoop, calls=%fused_computation.47 | loop fusion | flops 524288 | bytes 6291456 | tf_op jit(solution)/shard_map/concatenate | solution.py:14
  95.7 1.5 pad_maximum_fusion.5
  98.1 45.6 %reduce-scatter.5.cloned.1.call-done = f32[2,32,2048]{2,1,0:T(8,128)} async-done(((f32[2,128,2048]{2,1,0:T(8,128)}), f32[2,32,2048]{2,1,0:T(8,128)}) %reduce-scatter.5.cloned.1.call-update) | async-done | bytes 524304 | tf_op jit(solution)/shard_map/reduce_scatter | solution.py:20
  144.3 40.2 %psum.22 = f32[]{:T(128)} all-reduce(f32[]{:T(128)} %bitcast.7), channel_id=1, replica_groups=mesh['ev'=8,'st'=4] {'ev','st'}, use_global_device_ids=true, to_apply=%region_9.10 | all-reduce | flops 1 | bytes 8 | tf_op jit(solution)/shard_map/psum | solution.py:33
  185.3 0.8 copy.14
  186.1 12.9 %psum.25 = f32[2,32]{1,0:T(2,128)S(1)} all-reduce(f32[2,32]{1,0:T(2,128)S(1)} %copy.14), channel_id=1, replica_groups=mesh['ev'=8,'st'=4] {'ev'}, use_global_device_ids=true, to_apply=%region_10.11 | all-reduce | flops 64 | bytes 512 | tf_op jit(solution)/shard_map/psum | solution.py:18
  199.0 1.2 fusion.23
  200.2 21.0 %all-reduce.2.cloned.1.call-done = f32[2,32,2048]{2,1,0:T(8,128)} async-done(((f32[2,32,2048]{2,1,0:T(8,128)}), f32[2,32,2048]{2,1,0:T(8,128)}) %all-reduce.2.cloned.1.call-update) | async-done | bytes 524304 | tf_op jit(solution)/shard_map/psum | solution.py:18
  221.2 2.5 %fusion.22 = f32[32,2048]{1,0:T(8,128)} fusion(f32[2,32,2048]{2,1,0:T(8,128)} %all-reduce.2.cloned.1.call-done, f32[]{:T(128)S(6)} %sub.51, f32[]{:T(128)} %psum.22), kind=kLoop, calls=%fused_computation.51 | loop fusion | flops 262144 | bytes 786440 | tf_op jit(solution)/shard_map/mul | solution.py:96
  (93 shorter events, 18.9 us)
Async XLA Ops:
  7.2 1.7 copy-start.5
  7.2 1.7 copy-start.4
  7.2 136.5 %reduce-scatter.5.cloned.1.call-start = ((), (), s32[]{:S(2)}) async-start(), calls=%async_computation.2 | async-start | bytes 2621440 | tf_op jit(solution)/shard_map/reduce_scatter | solution.py:20
  8.8 0.7 copy-start.3
  8.8 0.8 copy-start.2
  14.0 2.2 copy-start
  18.1 1.9 copy-start.1
  24.4 2.2 copy-start
  28.5 1.9 copy-start.1
  34.9 2.2 copy-start
  38.9 1.9 copy-start.1
  45.3 2.2 copy-start
  49.3 1.9 copy-start.1
  55.7 2.2 copy-start
  59.7 1.9 copy-start.1
  66.1 2.2 copy-start
  70.2 1.9 copy-start.1
  76.5 2.2 copy-start
  80.6 1.9 copy-start.1
  86.9 2.2 copy-start
  91.0 1.9 copy-start.1
  97.2 88.1 %reduce-scatter.7.cloned.1.call-start = ((), (), s32[]{:S(2)}) async-start(), calls=%async_computation.4 | async-start | bytes 81920
  98.0 123.2 %all-reduce.2.cloned.1.call-start = ((), (), s32[]{:S(2)}) async-start(), calls=%async_computation.3 | async-start | bytes 1048576 | tf_op jit(solution)/shard_map/psum | solution.py:18
Sparse Core Ops, SparseCore 0:
  97.3 46.3 reduce-scatter.4
  146.5 18.4 reduce-scatter.6
  168.1 53.0 all-reduce.1
where the time goes:
time: 231 us; the launch traced here: 230 us
  waiting for transfers between devices  66.7 us (29%)
  blocking collectives  53.2 us (23%)
  other arithmetic  47.1 us (20%)
  local copies, waits for them, and re-layouts  26.6 us (12%)
  matrix products  20.7 us (9%)
  between operations  15.2 us (7%)
    reduce_scatter x1, waiting for transfers between devices, reduce_all(): lax.psum_scatter(whole[0], 'st', scatter_dimension=1, tiled=True)  45.6 us
    psum x1, blocking collectives, shards(): n_data = lax.psum(data_rows.astype(jnp.float32)[0], ('ev', 'st'))  40.2 us
    another operation x8, other arithmetic  23.9 us
    while x32, local copies, waits for them, and re-layouts  23.1 us
    psum x1, waiting for transfers between devices, reduce_all(): whole = lax.psum((grads, sums), 'ev')  21 us
    dot_general x8, matrix products, block_step(): lax.dot_general(split, dressed, (((0,), (0,)), ((), ())), preferred_eleme...  15 us
    psum x1, blocking collectives, reduce_all(): whole = lax.psum((grads, sums), 'ev')  12.9 us
    mul x8, other arithmetic, block_step(): offset = wave_square[None, :] - (mass * mass)[:, None]  6.13 us
  transfers between devices with their start and end apart: 3, of which 2 were waited for; matrix products, arithmetic and copies ran while one was open for 1% of the time, Pallas kernels for 0%

commit v1 on v0

v1 whole, which is shorter than its diff:
```python
import functools

import jax
import jax.numpy as jnp
from jax import lax
from jax.experimental import pallas as pl
from jax.experimental.pallas import tpu as pltpu
from jax.sharding import PartitionSpec as P

BLOCK = 512
ROWS = 16
LANES = 256
MESH = pl.DeviceIdType.MESH
F32 = jnp.float32
BF16 = jnp.bfloat16


def compute_kernel(
    limit_ref,
    pole_mass_ref,
    pole_width_ref,
    amp_ref,
    mass_ref,
    wave_ref,
    coef_ref,
    back_ref,
    grad_ref,
    sums_ref,
    mix,
    square,
    inverse,
    mass2,
    dressed,
    acc,
):
    step = pl.program_id(0)
    steps = pl.num_programs(0)
    waves = wave_ref.shape[1]
    starts = back_ref.shape[1]
    scale = waves ** (-0.5)
    limit = limit_ref[0]
    first = step * BLOCK

    @pl.when(step == 0)
    def _():
        which = wave_ref[...]
        peak = jnp.zeros(which.shape, F32)
        center = jnp.zeros(which.shape, F32)
        for k in range(pole_mass_ref.shape[0]):
            mass_k = pole_mass_ref[k]
            peak = jnp.where(which == k, mass_k * pole_width_ref[k], peak)
            center = jnp.where(which == k, mass_k * mass_k, center)
        square[...] = jnp.broadcast_to(center, square.shape)
        inverse[...] = jnp.broadcast_to(1.0 / peak, inverse.shape)
        coef_real = coef_ref[:, :waves].T
        coef_imag = coef_ref[:, waves:].T
        mix[:waves, :starts] = coef_real.astype(BF16)
        mix[:waves, starts:] = coef_imag.astype(BF16)
        mix[waves:, :starts] = (-coef_imag).astype(BF16)
        mix[waves:, starts:] = coef_real.astype(BF16)
        acc[...] = jnp.zeros_like(acc)
        sums_ref[...] = jnp.zeros_like(sums_ref)

    mass = mass_ref[0]
    mass2[...] = jnp.broadcast_to(mass * mass, (128, BLOCK)).T

    def dress(index, carry):
        row = pl.multiple_of(index * ROWS, ROWS)
        here = pl.ds(row, ROWS)
        m2 = mass2[here, :]
        m2 = jnp.concatenate([m2] * (LANES // 128), 1)
        for col in range(0, waves, LANES):
            real_cols = pl.ds(col, LANES)
            imag_cols = pl.ds(waves + col, LANES)
            sq = square[:, real_cols]
            inv = inverse[:, real_cols]
            sq = jnp.concatenate([sq] * (ROWS // 8), 0)
            inv = jnp.concatenate([inv] * (ROWS // 8), 0)
            u = (sq - m2) * inv
            denom = u * u + 1.0
            guess = pl.reciprocal(denom, approx=True)
            r = guess * (2.0 - denom * guess)
            amp_real = amp_ref[here, real_cols].astype(F32)
            amp_imag = amp_ref[here, imag_cols].astype(F32)
            dressed[here, real_cols] = ((amp_real * u - amp_imag) * r).astype(BF16)
            dressed[here, imag_cols] = ((amp_imag * u + amp_real) * r).astype(BF16)
        return carry

    lax.fori_loop(0, BLOCK // ROWS, dress, 0)

    value = jnp.dot(dressed[...], mix[...], preferred_element_type=F32) * scale
    val_real = value[:, :starts]
    val_imag = value[:, starts:]
    intensity = val_real * val_real + val_imag * val_imag + back_ref[...]
    is_data = first + lax.broadcasted_iota(jnp.int32, (BLOCK, starts), 0) < limit
    log_part = jnp.sum(jnp.where(is_data, jnp.log(intensity), 0.0), 0, keepdims=True)
    sim_part = jnp.sum(jnp.where(is_data, 0.0, intensity), 0, keepdims=True)
    sums_ref[0:1, :] += log_part
    sums_ref[1:2, :] += sim_part
    factor = jnp.where(is_data, -2.0 / intensity, 2.0)
    weighted = jnp.concatenate([factor * val_real, factor * val_imag], 1)
    both = jnp.concatenate([is_data, is_data], 1)

    @pl.when(first < limit)
    def _():
        w = jnp.where(both, weighted, 0.0).T.astype(BF16)
        acc[0] += jnp.dot(w, dressed[...], preferred_element_type=F32)

    @pl.when(first + BLOCK > limit)
    def _():
        w = jnp.where(both, 0.0, weighted).T.astype(BF16)
        acc[1] += jnp.dot(w, dressed[...], preferred_element_type=F32)

    @pl.when(step == steps - 1)
    def _():
        for part in range(2):
            grad_ref[part, :, :waves] = acc[part, :starts, :waves] + acc[part, starts:, waves:]
            grad_ref[part, :, waves:] = acc[part, starts:, :waves] - acc[part, :starts, waves:]


def compute(amplitudes, event_mass, data_rows, wave_shape, pole_mass, pole_width, coefficients, background):
    rows, wide = amplitudes.shape
    waves = wide // 2
    starts = coefficients.shape[0]
    smem = pl.BlockSpec(memory_space=pltpu.SMEM)
    return pl.pallas_call(
        compute_kernel,
        grid=(rows // BLOCK,),
        in_specs=[
            smem,
            smem,
            smem,
            pl.BlockSpec((BLOCK, wide), lambda i: (i, 0)),
            pl.BlockSpec((1, 1, BLOCK), lambda i: (i, 0, 0)),
            pl.BlockSpec((1, waves), lambda i: (0, 0)),
            pl.BlockSpec((starts, wide), lambda i: (0, 0)),
            pl.BlockSpec((1, starts), lambda i: (0, 0)),
        ],
        out_specs=[
            pl.BlockSpec((2, starts, wide), lambda i: (0, 0, 0)),
            pl.BlockSpec((8, starts), lambda i: (0, 0)),
        ],
        out_shape=[
            jax.ShapeDtypeStruct((2, starts, wide), F32),
            jax.ShapeDtypeStruct((8, starts), F32),
        ],
        scratch_shapes=[
            pltpu.VMEM((wide, 2 * starts), BF16),
            pltpu.VMEM((8, waves), F32),
            pltpu.VMEM((8, waves), F32),
            pltpu.VMEM((BLOCK, 128), F32),
            pltpu.VMEM((BLOCK, wide), BF16),
            pltpu.VMEM((2, 2 * starts, wide), F32),
        ],
        compiler_params=pltpu.CompilerParams(
            dimension_semantics=("arbitrary",), vmem_limit_bytes=48 * 1024 * 1024
        ),
        name="dress_and_fit",
    )(
        data_rows,
        pole_mass,
        pole_width,
        amplitudes,
        event_mass.reshape(rows // BLOCK, 1, BLOCK),
        wave_shape.reshape(1, waves),
        coefficients,
        background.reshape(1, starts),
    )


def reduce_kernel(
    n_ev,
    n_st,
    events,
    count_ref,
    grad_ref,
    sums_ref,
    out_ref,
    like_ref,
    tell,
    heard,
    mine,
    core_in,
    plane_sum,
    plane_in,
    st_sum,
    st_in,
    done,
    done_in,
    tell_send,
    tell_recv,
    core_send,
    core_recv,
    plane_send,
    plane_recv,
    st_send,
    st_recv,
    done_send,
    done_recv,
):
    ev = lax.axis_index("ev")
    st = lax.axis_index("st")
    n_dev = n_ev * n_st
    planes = n_ev // 2
    core = lax.rem(ev, 2)
    plane = ev // 2
    me = ev * n_st + st
    starts, wide = grad_ref.shape[1:]
    waves = wide // 2
    group = starts // n_st
    width = mine.shape[-1]
    chunks = wide // width

    def peer(offset):
        other = lax.rem(me + offset, n_dev)
        return other // n_st, lax.rem(other, n_st)

    barrier = pltpu.get_barrier_semaphore()
    for offset in range(1, n_dev):
        pl.semaphore_signal(barrier, inc=1, device_id=peer(offset), device_id_type=MESH)

    lane = lax.broadcasted_iota(jnp.int32, (1, 128), 1)
    count = jnp.full((1, 128), count_ref[0], jnp.int32).astype(F32)
    logs = sums_ref[0:1, :]
    sims = sums_ref[1:2, :]
    for z in range(n_st):
        log_row = pltpu.roll(logs, (128 - z * group) % 128, 1) if z else logs
        sim_row = pltpu.roll(sims, (128 + group - z * group) % 128, 1)
        row = jnp.where(lane < group, log_row, jnp.where(lane < 2 * group, sim_row, count))
        tell[z, 0:1, :] = row

    pl.semaphore_wait(barrier, n_dev - 1)

    told = []
    for offset in range(1, n_dev):
        to_ev, to_st = peer(offset)
        copy = pltpu.make_async_remote_copy(
            src_ref=tell.at[to_st, pl.ds(0, 1), :],
            dst_ref=heard.at[me, pl.ds(0, 1), :],
            send_sem=tell_send.at[offset],
            recv_sem=tell_recv.at[me],
            device_id=(to_ev, to_st),
            device_id_type=MESH,
        )
        copy.start()
        told.append(copy)
    heard[me, 0:1, :] = tell[st, 0:1, :]
    for offset in range(1, n_dev):
        from_me = lax.rem(me + offset, n_dev)
        pltpu.make_async_remote_copy(
            src_ref=tell.at[0, pl.ds(0, 1), :],
            dst_ref=heard.at[from_me, pl.ds(0, 1), :],
            send_sem=tell_send.at[offset],
            recv_sem=tell_recv.at[from_me],
            device_id=peer(offset),
            device_id_type=MESH,
        ).wait_recv()
    total = heard[0, 0:1, :]
    for index in range(1, n_dev):
        total = total + heard[index, 0:1, :]
    n_data = jnp.sum(jnp.where(lane == 2 * group, total, 0.0), 1, keepdims=True)
    n_sim = events - n_data
    like_ref[...] = pltpu.roll(total, 128 - group, 1) / n_sim - total / n_data
    scale = waves ** 0.5
    by_data = jnp.broadcast_to(scale / n_data, (8, width))
    by_sim = jnp.broadcast_to(scale / n_sim, (8, width))

    def place(index):
        return 8 * (index // chunks), width * (index % chunks)

    for c in range(2):
        for p in range(planes):
            row, col = place(c * planes + p)
            for z in range(n_st):
                here = (pl.ds(z * group + row, 8), pl.ds(col, width))
                mine[c, p, z] = (
                    grad_ref[(0, *here)] * by_data + grad_ref[(1, *here)] * by_sim
                )

    first = pltpu.make_async_remote_copy(
        src_ref=mine.at[1 - core],
        dst_ref=core_in,
        send_sem=core_send,
        recv_sem=core_recv,
        device_id=(2 * plane + 1 - core, st),
        device_id_type=MESH,
    )
    first.start()
    first.wait_recv()
    plane_sum[...] = mine[core] + core_in[...]

    plane_copies = []
    for offset in range(1, planes):
        to = lax.rem(plane + offset, planes)
        copy = pltpu.make_async_remote_copy(
            src_ref=plane_sum.at[to],
            dst_ref=plane_in.at[offset],
            send_sem=plane_send.at[offset],
            recv_sem=plane_recv.at[offset],
            device_id=(2 * to + core, st),
            device_id_type=MESH,
        )
        copy.start()
        plane_copies.append(copy)
    part = plane_sum[plane]
    for offset in range(1, planes):
        plane_copies[offset - 1].wait_recv()
        part = part + plane_in[offset]
    st_sum[...] = part

    st_copies = []
    for offset in range(1, n_st):
        to = lax.rem(st + offset, n_st)
        copy = pltpu.make_async_remote_copy(
            src_ref=st_sum.at[to],
            dst_ref=st_in.at[offset],
            send_sem=st_send.at[offset],
            recv_sem=st_recv.at[offset],
            device_id=(ev, to),
            device_id_type=MESH,
        )
        copy.start()
        st_copies.append(copy)
    part = st_sum[st]
    for offset in range(1, n_st):
        st_copies[offset - 1].wait_recv()
        part = part + st_in[offset]
    done[...] = part

    slot = core * planes + plane
    done_copies = []
    for offset in range(1, n_ev):
        to = lax.rem(ev + offset, n_ev)
        copy = pltpu.make_async_remote_copy(
            src_ref=done,
            dst_ref=done_in.at[slot],
            send_sem=done_send.at[offset],
            recv_sem=done_recv.at[slot],
            device_id=(to, st),
            device_id_type=MESH,
        )
        copy.start()
        done_copies.append(copy)
    done_in[slot] = part
    for offset in range(1, n_ev):
        other = lax.rem(ev + offset, n_ev)
        other_slot = lax.rem(other, 2) * planes + other // 2
        pltpu.make_async_remote_copy(
            src_ref=done,
            dst_ref=done_in.at[other_slot],
            send_sem=done_send.at[offset],
            recv_sem=done_recv.at[other_slot],
            device_id=(other, st),
            device_id_type=MESH,
        ).wait_recv()
    for index in range(n_ev):
        row, col = place(index)
        out_ref[row : row + 8, col : col + width] = done_in[index]

    for copy in told + [first] + plane_copies + st_copies + done_copies:
        copy.wait_send()


def reduce_all(n_ev, n_st, events, data_rows, grads, sums):
    starts, wide = grads.shape[1:]
    group = starts // n_st
    planes = n_ev // 2
    width = group * wide // (8 * n_ev)
    n_dev = n_ev * n_st
    dma = pltpu.SemaphoreType.DMA
    vmem = pl.BlockSpec(memory_space=pltpu.VMEM)
    return pl.pallas_call(
        functools.partial(reduce_kernel, n_ev, n_st, events),
        in_specs=[pl.BlockSpec(memory_space=pltpu.SMEM), vmem, vmem],
        out_specs=[vmem, vmem],
        out_shape=[
            jax.ShapeDtypeStruct((group, wide), F32),
            jax.ShapeDtypeStruct((1, 128), F32),
        ],
        scratch_shapes=[
            pltpu.VMEM((n_st, 8, 128), F32),
            pltpu.VMEM((n_dev, 8, 128), F32),
            pltpu.VMEM((2, planes, n_st, 8, width), F32),
            pltpu.VMEM((planes, n_st, 8, width), F32),
            pltpu.VMEM((planes, n_st, 8, width), F32),
            pltpu.VMEM((planes, n_st, 8, width), F32),
            pltpu.VMEM((n_st, 8, width), F32),
            pltpu.VMEM((n_st, 8, width), F32),
            pltpu.VMEM((8, width), F32),
            pltpu.VMEM((n_ev, 8, width), F32),
            dma((n_dev,)),
            dma((n_dev,)),
            dma,
            dma,
            dma((planes,)),
            dma((planes,)),
            dma((n_st,)),
            dma((n_st,)),
            dma((n_ev,)),
            dma((n_ev,)),
        ],
        compiler_params=pltpu.CompilerParams(
            collective_id=0, has_side_effects=True, vmem_limit_bytes=32 * 1024 * 1024
        ),
        name="reduce_starts",
    )(data_rows, grads, sums)


def solution(mesh):
    n_ev = mesh.shape["ev"]
    n_st = mesh.shape["st"]

    def shards(
        amplitudes, event_mass, data_rows, wave_shape, pole_mass, pole_width, coefficients, background
    ):
        grads, sums = compute(
            amplitudes, event_mass, data_rows, wave_shape, pole_mass, pole_width, coefficients, background
        )
        events = amplitudes.shape[0] * n_ev * n_st
        gradient, like = reduce_all(n_ev, n_st, events, data_rows, grads, sums)
        return gradient, like[0, : coefficients.shape[0] // n_st]

    return jax.shard_map(
        shards,
        mesh=mesh,
        in_specs=(P(("ev", "st"), None), P(("ev", "st")), P(("ev", "st")), P(), P(), P(), P(), P()),
        out_specs=(P("st", None), P("st")),
        check_vma=False,
    )
```

time: 231 us -> 65.7 us (0.28)
  waiting for transfers between devices: 66.7 us -> 0 us
  Pallas kernels: 0 us -> 58.2 us
  blocking collectives: 53.2 us -> 0 us
  other arithmetic: 47.1 us -> 0 us
  local copies, waits for them, and re-layouts: 26.6 us -> 5.8 us
  matrix products: 20.7 us -> 0 us
  between operations: 15.2 us -> 1.31 us
    pallas_call x0 -> x2, Pallas kernels: none -> 58.2 us  [the longest x1 30.2 us: reduce_all(): pl.pallas_call(functools.partial(reduce_kernel, n_ev, n_st, events), in_s...]
    psum x2 -> x0, blocking collectives: 53.2 us -> none  [the longest x1 40.2 us: shards(): n_data = lax.psum(data_rows.astype(jnp.float32)[0], ('ev', 'st'))]
    reduce_scatter x1 -> x0, waiting for transfers between devices: 45.6 us -> none  [reduce_all(): lax.psum_scatter(whole[0], 'st', scatter_dimension=1, tiled=True)]
    another operation x10 -> x0, other arithmetic: 25.4 us -> none
    while x32 -> x0, local copies, waits for them, and re-layouts: 23.1 us -> none
    psum x1 -> x0, waiting for transfers between devices: 21 us -> none  [reduce_all(): whole = lax.psum((grads, sums), 'ev')]
    dot_general x16 -> x0, matrix products: 20.7 us -> none  [the longest x8 15 us: block_step(): lax.dot_general(split, dressed, (((0,), (0,)), ((), ())), preferred_eleme...]
    mul x11 -> x0, other arithmetic: 8.79 us -> none  [the longest x8 6.13 us: block_step(): offset = wave_square[None, :] - (mass * mass)[:, None]]
  transfers between devices with their start and end apart: 3 -> 0, of which waited for: 2 -> 0; matrix products, arithmetic and copies ran while one was open for 1% -> 0% of each run, Pallas kernels for 0% -> 0%
where the time goes in v1:
time: 65.7 us; the launch traced here: 65.4 us
  Pallas kernels  58.2 us (89%)
  local copies, waits for them, and re-layouts  5.8 us (9%)
  between operations  1.31 us (2%)
    pallas_call x1, Pallas kernels, reduce_all(): pl.pallas_call(functools.partial(reduce_kernel, n_ev, n_st, events), in_s...  30.2 us
    pallas_call x1, Pallas kernels, compute(): pl.pallas_call(compute_kernel, grid=(rows // BLOCK,), in_specs=[smem, sme...  28.1 us
    unnamed x13, local copies, waits for them, and re-layouts  5.29 us

profile of v1, /device:TPU:0, one launch (start us, length us, event | category | flops | bytes accessed | tf_op | source)
XLA Modules:
  0.0 65.4 jit_solution(11243103243519369160)
XLA Ops:
  1.3 0.0 copy-start
  1.3 1.2 %copy-done = f32[128,2048]{1,0:T(8,128)S(1)} copy-done((f32[128,2048]{1,0:T(8,128)S(1)}, f32[128,2048]{1,0:T(8,128)}, u32[]{:S(2)}) %copy-start) | copy-done | bytes 1048600
  2.5 0.0 copy-start.1
  2.5 0.7 %copy-done.1 = f32[4096]{0:T(1024)S(1)} copy-done((f32[4096]{0:T(1024)S(1)}, f32[4096]{0:T(1024)}, u32[]{:S(2)}) %copy-start.1) | copy-done | bytes 16408
  3.2 0.0 copy-start.2
  3.2 0.7 %copy-done.2 = s32[1024]{0:T(1024)S(1)} copy-done((s32[1024]{0:T(1024)S(1)}, s32[1024]{0:T(1024)}, u32[]{:S(2)}) %copy-start.2) | copy-done | bytes 4120
  3.9 0.0 copy-start.3
  3.9 0.7 copy-done.3
  4.6 0.0 copy-start.4
  4.6 0.7 copy-done.4
  5.2 0.0 copy-start.5
  5.2 0.7 copy-done.5
  5.9 28.1 %dress_and_fit.1 = (f32[2,128,2048]{2,1,0:T(8,128)S(1)}, f32[8,128]{1,0:T(8,128)S(1)}) custom-call(s32[1]{0:T(128)S(6)} %copy.11.limit_ref.count_ref, f32[32]{0:T(128)S(1)} %copy-done.3, f32[32]{0:T(128)S(1)} %copy-done.4, bf16[4096,2048]{1,0:T(8,128)(2,1)} %amp_ref.1, f32[8,1,512]{2,1,0:T(1,128)S(1)} %bitcast.5, s32[1,1024]{1,0:T(1,128)S(1)} %bitcast.6, ...), custom_call_target="tpu_custom_call" | custom-call | tf_op jit(solution)/shard_map/dress_and_fit/pallas_call | solution.py:126
  34.0 30.2 %reduce_starts.1 = (f32[32,2048]{1,0:T(8,128)S(1)}, f32[1,128]{1,0:T(1,128)S(1)}) custom-call(s32[1]{0:T(128)S(6)} %copy.11.limit_ref.count_ref, f32[2,128,2048]{2,1,0:T(8,128)S(1)} %get-tuple-element.6.grad_ref, f32[8,128]{1,0:T(8,128)S(1)} %get-tuple-element.7.sums_ref), custom_call_target="tpu_custom_call" | custom-call | tf_op jit(solution)/shard_map/reduce_starts/pallas_call | solution.py:372
  64.1 0.5 slice_bitcast_fusion
  64.7 0.7 %copy.12 = f32[32,2048]{1,0:T(8,128)} copy(f32[32,2048]{1,0:T(8,128)S(1)} %get-tuple-element.12) | data formatting | bytes 524288
Async XLA Ops:
  1.3 1.2 %copy-start = (f32[128,2048]{1,0:T(8,128)S(1)}, f32[128,2048]{1,0:T(8,128)}, u32[]{:S(2)}) copy-start(f32[128,2048]{1,0:T(8,128)} %coef_ref.1) | copy-start | bytes 3145732
  2.5 0.7 %copy-start.1 = (f32[4096]{0:T(1024)S(1)}, f32[4096]{0:T(1024)}, u32[]{:S(2)}) copy-start(f32[4096]{0:T(1024)} %param.9) | copy-start | bytes 49156
  3.2 0.7 %copy-start.2 = (s32[1024]{0:T(1024)S(1)}, s32[1024]{0:T(1024)}, u32[]{:S(2)}) copy-start(s32[1024]{0:T(1024)} %param.11) | copy-start | bytes 12292
  3.9 0.7 %copy-start.3 = (f32[32]{0:T(128)S(1)}, f32[32]{0:T(128)}, u32[]{:S(2)}) copy-start(f32[32]{0:T(128)} %pole_mass_ref.1) | copy-start | bytes 388
  4.6 0.7 %copy-start.4 = (f32[32]{0:T(128)S(1)}, f32[32]{0:T(128)}, u32[]{:S(2)}) copy-start(f32[32]{0:T(128)} %pole_width_ref.1) | copy-start | bytes 388
  5.2 0.7 %copy-start.5 = (f32[128]{0:T(128)S(1)}, f32[128]{0:T(128)}, u32[]{:S(2)}) copy-start(f32[128]{0:T(128)} %param.15) | copy-start | bytes 1540

commit v2 on v0

v2 whole, which is shorter than its diff:
```python
import functools

import jax
import jax.numpy as jnp
from jax import lax
from jax.experimental import pallas as pl
from jax.experimental.pallas import tpu as pltpu
from jax.sharding import PartitionSpec as P

BLOCK = 512
ROWS = 16
LANES = 256
MESH = pl.DeviceIdType.MESH
F32 = jnp.float32
BF16 = jnp.bfloat16


def fit_kernel(
    n_ev,
    n_st,
    parts,
    limit_hbm,
    pole_mass_hbm,
    pole_width_hbm,
    amp_hbm,
    mass_hbm,
    wave_hbm,
    coef_hbm,
    back_hbm,
    out_ref,
    like_ref,
    limit_ref,
    pole_mass_ref,
    pole_width_ref,
    amp_ref,
    mass_ref,
    wave_ref,
    coef_ref,
    back_ref,
    mix,
    square,
    inverse,
    mass2,
    sums,
    raw,
    weights,
    count_tell,
    count_heard,
    tell,
    heard,
    mine,
    core_in,
    plane_sum,
    plane_in,
    st_sum,
    st_in,
    done,
    done_in,
    load_sem,
    amp_sem,
    count_send,
    count_recv,
    tell_send,
    tell_recv,
    core_send,
    core_recv,
    plane_send,
    plane_recv,
    st_send,
    st_recv,
    done_send,
    done_recv,
):
    ev = lax.axis_index("ev")
    st = lax.axis_index("st")
    n_dev = n_ev * n_st
    planes = n_ev // 2
    core = lax.rem(ev, 2)
    plane = ev // 2
    me = ev * n_st + st
    rows, wide = amp_ref.shape
    waves = wide // 2
    starts = back_ref.shape[1]
    group = starts // n_st
    events = rows * n_dev
    blocks = rows // BLOCK
    scale = waves ** (-0.5)
    width = mine.shape[-1]
    part_waves = waves // parts
    per = 2 * part_waves // width

    def peer(offset):
        other = lax.rem(me + offset, n_dev)
        return other // n_st, lax.rem(other, n_st)

    loads = [
        pltpu.make_async_copy(src, dst, load_sem.at[index])
        for index, (src, dst) in enumerate(
            [
                (coef_hbm, coef_ref),
                (wave_hbm, wave_ref),
                (limit_hbm, limit_ref),
                (pole_mass_hbm, pole_mass_ref),
                (pole_width_hbm, pole_width_ref),
                (mass_hbm, mass_ref),
                (back_hbm, back_ref),
            ]
        )
    ]
    for load in loads:
        load.start()

    def fetch(index):
        here = pl.ds(pl.multiple_of(index * BLOCK, BLOCK), BLOCK)
        return pltpu.make_async_copy(amp_hbm.at[here, :], amp_ref.at[here, :], amp_sem.at[index])

    for index in range(blocks):
        fetch(index).start()

    barrier = pltpu.get_barrier_semaphore()
    for offset in range(1, n_dev):
        pl.semaphore_signal(barrier, inc=1, device_id=peer(offset), device_id_type=MESH)

    for load in loads:
        load.wait()
    limit = limit_ref[0]
    which = wave_ref[...]
    peak = jnp.zeros(which.shape, F32)
    center = jnp.zeros(which.shape, F32)
    for k in range(pole_mass_ref.shape[0]):
        mass_k = pole_mass_ref[k]
        peak = jnp.where(which == k, mass_k * pole_width_ref[k], peak)
        center = jnp.where(which == k, mass_k * mass_k, center)
    square[...] = jnp.broadcast_to(center, square.shape)
    inverse[...] = jnp.broadcast_to(1.0 / peak, inverse.shape)
    coef_real = coef_ref[:, :waves].T
    coef_imag = coef_ref[:, waves:].T
    mix[:waves, :starts] = coef_real.astype(BF16)
    mix[:waves, starts:] = coef_imag.astype(BF16)
    mix[waves:, :starts] = (-coef_imag).astype(BF16)
    mix[waves:, starts:] = coef_real.astype(BF16)
    sums[...] = jnp.zeros_like(sums)
    count_tell[0:1, :] = jnp.full((1, 128), limit, jnp.int32).astype(F32)

    pl.semaphore_wait(barrier, n_dev - 1)

    def count_copy(offset, slot):
        return pltpu.make_async_remote_copy(
            src_ref=count_tell.at[pl.ds(0, 1), :],
            dst_ref=count_heard.at[slot, pl.ds(0, 1), :],
            send_sem=count_send.at[offset],
            recv_sem=count_recv.at[slot],
            device_id=peer(offset),
            device_id_type=MESH,
        )

    for offset in range(1, n_dev):
        count_copy(offset, me).start()
    count_heard[me, 0:1, :] = count_tell[0:1, :]

    def block_step(step, carry):
        first = pl.multiple_of(step * BLOCK, BLOCK)
        fetch(step).wait()
        mass = mass_ref[step]
        mass2[...] = jnp.broadcast_to(mass * mass, (128, BLOCK)).T

        def dress(index, carry):
            row = pl.multiple_of(index * ROWS, ROWS)
            here = pl.ds(pl.multiple_of(first + row, ROWS), ROWS)
            m2 = mass2[pl.ds(row, ROWS), :]
            m2 = jnp.concatenate([m2] * (LANES // 128), 1)
            for col in range(0, waves, LANES):
                real_cols = pl.ds(col, LANES)
                imag_cols = pl.ds(waves + col, LANES)
                sq = jnp.concatenate([square[:, real_cols]] * (ROWS // 8), 0)
                inv = jnp.concatenate([inverse[:, real_cols]] * (ROWS // 8), 0)
                u = (sq - m2) * inv
                denom = u * u + 1.0
                guess = pl.reciprocal(denom, approx=True)
                r = guess * (2.0 - denom * guess)
                amp_real = amp_ref[here, real_cols].astype(F32)
                amp_imag = amp_ref[here, imag_cols].astype(F32)
                amp_ref[here, real_cols] = ((amp_real * u - amp_imag) * r).astype(BF16)
                amp_ref[here, imag_cols] = ((amp_imag * u + amp_real) * r).astype(BF16)
            return carry

        lax.fori_loop(0, BLOCK // ROWS, dress, 0)

        dressed = amp_ref[pl.ds(first, BLOCK), :]
        value = jnp.dot(dressed, mix[...], preferred_element_type=F32) * scale
        val_real = value[:, :starts]
        val_imag = value[:, starts:]
        intensity = val_real * val_real + val_imag * val_imag + back_ref[...]
        is_data = first + lax.broadcasted_iota(jnp.int32, (BLOCK, starts), 0) < limit
        sums[0:1, :] += jnp.sum(jnp.where(is_data, jnp.log(intensity), 0.0), 0, keepdims=True)
        sums[1:2, :] += jnp.sum(jnp.where(is_data, 0.0, intensity), 0, keepdims=True)
        factor = jnp.where(is_data, -2.0 / intensity, 2.0)
        raw[step] = jnp.concatenate([factor * val_real, factor * val_imag], 1).T
        return carry

    lax.fori_loop(0, blocks, block_step, 0)

    lane = lax.broadcasted_iota(jnp.int32, (1, 128), 1)
    for z in range(n_st):
        log_row = pltpu.roll(sums[0:1, :], 128 - z * group, 1) if z else sums[0:1, :]
        sim_row = pltpu.roll(sums[1:2, :], (128 + group - z * group) % 128, 1) if z != 1 else sums[1:2, :]
        tell[z, 0:1, :] = jnp.where(lane < group, log_row, sim_row)

    def tell_copy(offset, slot):
        to_ev, to_st = peer(offset)
        return pltpu.make_async_remote_copy(
            src_ref=tell.at[to_st, pl.ds(0, 1), :],
            dst_ref=heard.at[slot, pl.ds(0, 1), :],
            send_sem=tell_send.at[offset],
            recv_sem=tell_recv.at[slot],
            device_id=(to_ev, to_st),
            device_id_type=MESH,
        )

    for offset in range(1, n_dev):
        tell_copy(offset, me).start()
    heard[me, 0:1, :] = tell[st, 0:1, :]

    for offset in range(1, n_dev):
        count_copy(offset, lax.rem(me + offset, n_dev)).wait_recv()
    n_data = count_heard[0, 0:1, :]
    for index in range(1, n_dev):
        n_data = n_data + count_heard[index, 0:1, :]
    n_sim = events - n_data
    ratio = jnp.broadcast_to((n_sim / n_data)[:, 0:1], (2 * starts, BLOCK))
    final = jnp.broadcast_to((waves * scale / n_sim)[:, 0:1], (8, width))

    def scale_step(step, carry):
        first = step * BLOCK
        is_data = first + lax.broadcasted_iota(jnp.int32, (2 * starts, BLOCK), 1) < limit
        w = raw[step]
        here = pl.ds(pl.multiple_of(first, BLOCK), BLOCK)
        weights[:, here] = jnp.where(is_data, w * ratio, w).astype(BF16)
        return carry

    lax.fori_loop(0, blocks, scale_step, 0)

    def place(index):
        return 8 * (index // per), width * (index % per)

    def core_copy(part):
        return pltpu.make_async_remote_copy(
            src_ref=mine.at[part, 1 - core],
            dst_ref=core_in.at[part],
            send_sem=core_send.at[part],
            recv_sem=core_recv.at[part],
            device_id=(2 * plane + 1 - core, st),
            device_id_type=MESH,
        )

    def plane_copy(part, offset):
        to = lax.rem(plane + offset, planes)
        return pltpu.make_async_remote_copy(
            src_ref=plane_sum.at[part, to],
            dst_ref=plane_in.at[part, offset],
            send_sem=plane_send.at[part, offset],
            recv_sem=plane_recv.at[part, offset],
            device_id=(2 * to + core, st),
            device_id_type=MESH,
        )

    def st_copy(part, offset):
        to = lax.rem(st + offset, n_st)
        return pltpu.make_async_remote_copy(
            src_ref=st_sum.at[part, to],
            dst_ref=st_in.at[part, offset],
            send_sem=st_send.at[part, offset],
            recv_sem=st_recv.at[part, offset],
            device_id=(ev, to),
            device_id_type=MESH,
        )

    def done_copy(part, offset, slot):
        return pltpu.make_async_remote_copy(
            src_ref=done.at[part],
            dst_ref=done_in.at[part, slot],
            send_sem=done_send.at[part, offset],
            recv_sem=done_recv.at[part, slot],
            device_id=(lax.rem(ev + offset, n_ev), st),
            device_id_type=MESH,
        )

    slot = core * planes + plane

    def make_part(part):
        real_cols = pl.ds(part * part_waves, part_waves)
        imag_cols = pl.ds(waves + part * part_waves, part_waves)
        by_real = jnp.dot(weights[...], amp_ref[:, real_cols], preferred_element_type=F32)
        by_imag = jnp.dot(weights[...], amp_ref[:, imag_cols], preferred_element_type=F32)
        grad = jnp.concatenate(
            [by_real[:starts] + by_imag[starts:], by_real[starts:] - by_imag[:starts]], 1
        )
        for c in range(2):
            for p in range(planes):
                row, col = place(c * planes + p)
                for z in range(n_st):
                    at = z * group + row
                    mine[part, c, p, z] = grad[at : at + 8, col : col + width] * final
        core_copy(part).start()

    def plane_stage(part):
        core_copy(part).wait_recv()
        plane_sum[part] = mine[part, core] + core_in[part]
        for offset in range(1, planes):
            plane_copy(part, offset).start()

    def st_stage(part):
        total = plane_sum[part, plane]
        for offset in range(1, planes):
            plane_copy(part, offset).wait_recv()
            total = total + plane_in[part, offset]
        st_sum[part] = total
        for offset in range(1, n_st):
            st_copy(part, offset).start()

    def done_stage(part):
        total = st_sum[part, st]
        for offset in range(1, n_st):
            st_copy(part, offset).wait_recv()
            total = total + st_in[part, offset]
        done[part] = total
        for offset in range(1, n_ev):
            done_copy(part, offset, slot).start()
        done_in[part, slot] = total

    for tick in range(parts + 3):
        if tick < parts:
            make_part(tick)
        if 0 <= tick - 3 < parts:
            done_stage(tick - 3)
        if 0 <= tick - 2 < parts:
            st_stage(tick - 2)
        if 0 <= tick - 1 < parts:
            plane_stage(tick - 1)

    for offset in range(1, n_dev):
        tell_copy(offset, lax.rem(me + offset, n_dev)).wait_recv()
    total = heard[0, 0:1, :]
    for index in range(1, n_dev):
        total = total + heard[index, 0:1, :]
    like_ref[...] = pltpu.roll(total, 128 - group, 1) / n_sim - total / n_data

    for part in range(parts):
        for offset in range(1, n_ev):
            other = lax.rem(ev + offset, n_ev)
            done_copy(part, offset, lax.rem(other, 2) * planes + other // 2).wait_recv()
        for index in range(n_ev):
            row, col = place(index)
            at = part * part_waves + col
            if col >= part_waves:
                at += waves - part_waves
            out_ref[row : row + 8, at : at + width] = done_in[part, index]

    for offset in range(1, n_dev):
        count_copy(offset, me).wait_send()
        tell_copy(offset, me).wait_send()
    for part in range(parts):
        core_copy(part).wait_send()
        for offset in range(1, planes):
            plane_copy(part, offset).wait_send()
        for offset in range(1, n_st):
            st_copy(part, offset).wait_send()
        for offset in range(1, n_ev):
            done_copy(part, offset, slot).wait_send()


def solution(mesh):
    n_ev = mesh.shape["ev"]
    n_st = mesh.shape["st"]
    n_dev = n_ev * n_st
    planes = n_ev // 2
    dma = pltpu.SemaphoreType.DMA
    vmem = pltpu.VMEM
    smem = pltpu.SMEM

    def shards(
        amplitudes, event_mass, data_rows, wave_shape, pole_mass, pole_width, coefficients, background
    ):
        rows, wide = amplitudes.shape
        waves = wide // 2
        starts = coefficients.shape[0]
        shapes = pole_mass.shape[0]
        group = starts // n_st
        parts = 4
        while (group // 8) * (wide // parts // 128) % n_ev:
            parts //= 2
        width = group * wide // (8 * n_ev * parts)
        blocks = rows // BLOCK
        piece = (8, width)
        gradient, like = pl.pallas_call(
            functools.partial(fit_kernel, n_ev, n_st, parts),
            in_specs=[pl.BlockSpec(memory_space=pltpu.HBM)] * 8,
            out_specs=[pl.BlockSpec(memory_space=pltpu.VMEM)] * 2,
            out_shape=[
                jax.ShapeDtypeStruct((group, wide), F32),
                jax.ShapeDtypeStruct((1, 128), F32),
            ],
            scratch_shapes=[
                smem((1,), jnp.int32),
                smem((shapes,), F32),
                smem((shapes,), F32),
                vmem((rows, wide), BF16),
                vmem((blocks, 1, BLOCK), F32),
                vmem((1, waves), jnp.int32),
                vmem((starts, wide), F32),
                vmem((1, starts), F32),
                vmem((wide, 2 * starts), BF16),
                vmem((8, waves), F32),
                vmem((8, waves), F32),
                vmem((BLOCK, 128), F32),
                vmem((8, 128), F32),
                vmem((blocks, 2 * starts, BLOCK), F32),
                vmem((2 * starts, rows), BF16),
                vmem((8, 128), F32),
                vmem((n_dev, 8, 128), F32),
                vmem((n_st, 8, 128), F32),
                vmem((n_dev, 8, 128), F32),
                vmem((parts, 2, planes, n_st, *piece), F32),
                vmem((parts, planes, n_st, *piece), F32),
                vmem((parts, planes, n_st, *piece), F32),
                vmem((parts, planes, n_st, *piece), F32),
                vmem((parts, n_st, *piece), F32),
                vmem((parts, n_st, *piece), F32),
                vmem((parts, *piece), F32),
                vmem((parts, n_ev, *piece), F32),
                dma((7,)),
                dma((blocks,)),
                dma((n_dev,)),
                dma((n_dev,)),
                dma((n_dev,)),
                dma((n_dev,)),
                dma((parts,)),
                dma((parts,)),
                dma((parts, planes)),
                dma((parts, planes)),
                dma((parts, n_st)),
                dma((parts, n_st)),
                dma((parts, n_ev)),
                dma((parts, n_ev)),
            ],
            compiler_params=pltpu.CompilerParams(
                collective_id=0, has_side_effects=True, vmem_limit_bytes=56 * 1024 * 1024
            ),
            name="fit_all",
        )(
            data_rows,
            pole_mass,
            pole_width,
            amplitudes,
            event_mass.reshape(blocks, 1, BLOCK),
            wave_shape.reshape(1, waves),
            coefficients,
            background.reshape(1, starts),
        )
        return gradient, like[0, :group]

    return jax.shard_map(
        shards,
        mesh=mesh,
        in_specs=(P(("ev", "st"), None), P(("ev", "st")), P(("ev", "st")), P(), P(), P(), P(), P()),
        out_specs=(P("st", None), P("st")),
        check_vma=False,
    )
```

time: 231 us -> 64.5 us (0.28)
  waiting for transfers between devices: 66.7 us -> 0 us
  Pallas kernels: 0 us -> 60.3 us
  blocking collectives: 53.2 us -> 0 us
  other arithmetic: 47.1 us -> 0 us
  local copies, waits for them, and re-layouts: 26.6 us -> 2.8 us
  matrix products: 20.7 us -> 0 us
  between operations: 15.2 us -> 1.29 us
    pallas_call x0 -> x1, Pallas kernels: none -> 60.3 us  [shards(): pl.pallas_call(functools.partial(fit_kernel, n_ev, n_st, parts), in_specs...]
    psum x2 -> x0, blocking collectives: 53.2 us -> none  [the longest x1 40.2 us: shards(): n_data = lax.psum(data_rows.astype(jnp.float32)[0], ('ev', 'st'))]
    reduce_scatter x1 -> x0, waiting for transfers between devices: 45.6 us -> none  [reduce_all(): lax.psum_scatter(whole[0], 'st', scatter_dimension=1, tiled=True)]
    another operation x10 -> x0, other arithmetic: 25.4 us -> none
    while x32 -> x0, local copies, waits for them, and re-layouts: 23.1 us -> none
    psum x1 -> x0, waiting for transfers between devices: 21 us -> none  [reduce_all(): whole = lax.psum((grads, sums), 'ev')]
    dot_general x16 -> x0, matrix products: 20.7 us -> none  [the longest x8 15 us: block_step(): lax.dot_general(split, dressed, (((0,), (0,)), ((), ())), preferred_eleme...]
    mul x11 -> x0, other arithmetic: 8.79 us -> none  [the longest x8 6.13 us: block_step(): offset = wave_square[None, :] - (mass * mass)[:, None]]
  transfers between devices with their start and end apart: 3 -> 0, of which waited for: 2 -> 0; matrix products, arithmetic and copies ran while one was open for 1% -> 0% of each run, Pallas kernels for 0% -> 0%
where the time goes in v2:
time: 64.5 us; the launch traced here: 64.3 us
  Pallas kernels  60.3 us (93%)
  local copies, waits for them, and re-layouts  2.8 us (4%)
  between operations  1.29 us (2%)
    pallas_call x1, Pallas kernels, shards(): pl.pallas_call(functools.partial(fit_kernel, n_ev, n_st, parts), in_specs...  60.3 us
    unnamed x1, local copies, waits for them, and re-layouts  1.67 us

profile of v2, /device:TPU:0, one launch (start us, length us, event | category | flops | bytes accessed | tf_op | source)
XLA Modules:
  0.0 64.3 jit_solution(4747645556763467098)
XLA Ops:
  1.3 60.3 %fit_all.1 = (f32[32,2048]{1,0:T(8,128)}, f32[1,128]{1,0:T(1,128)}) custom-call(s32[1]{0:T(128)S(6)} %copy.11.limit_hbm, f32[32]{0:T(128)} %pole_mass_hbm.1, f32[32]{0:T(128)} %pole_width_hbm.1, bf16[4096,2048]{1,0:T(8,128)(2,1)} %amp_hbm.1, f32[8,1,512]{2,1,0:T(1,128)} %bitcast.5, s32[1,1024]{1,0:T(1,128)} %bitcast.6, f32[128,2048]{1,0:T(8,128)} %coef_hbm.1, ...), custom_call_target="tpu_custom_call" | custom-call | tf_op jit(solution)/shard_map/fit_all/pallas_call | solution.py:395
  61.5 1.1 %slice_bitcast_fusion = f32[32]{0:T(128)} fusion(f32[1,128]{1,0:T(1,128)} %get-tuple-element.5), kind=kLoop, calls=%fused_computation | loop fusion | bytes 256 | tf_op jit(solution)/shard_map/squeeze | solution.py:460
  62.7 1.7 %copy.12 = f32[32,2048]{1,0:T(8,128)} copy(f32[32,2048]{1,0:T(8,128)} %get-tuple-element.8) | data formatting | bytes 524288

commit v3 on v2

--- a/solution.py
+++ b/solution.py
@@ -44,10 +44,10 @@
     sums,
     raw,
     weights,
-    count_tell,
-    count_heard,
-    tell,
-    heard,
+    tiny,
+    tiny_core,
+    tiny_plane,
+    tiny_st,
     mine,
     core_in,
     plane_sum,
@@ -58,10 +58,8 @@
     done_in,
     load_sem,
     amp_sem,
-    count_send,
-    count_recv,
-    tell_send,
-    tell_recv,
+    tiny_send,
+    tiny_recv,
     core_send,
     core_recv,
     plane_send,
@@ -76,8 +74,7 @@
     n_dev = n_ev * n_st
     planes = n_ev // 2
     core = lax.rem(ev, 2)
-    plane = ev // 2
-    me = ev * n_st + st
+    plane = lax.div(ev, 2)
     rows, wide = amp_ref.shape
     waves = wide // 2
     starts = back_ref.shape[1]
@@ -89,9 +86,17 @@
     part_waves = waves // parts
     per = 2 * part_waves // width
 
-    def peer(offset):
-        other = lax.rem(me + offset, n_dev)
-        return other // n_st, lax.rem(other, n_st)
+    partner = (ev + 1 - 2 * core, st)
+    plane_at = [lax.rem(plane + offset, planes) for offset in range(planes)]
+    plane_to = [(2 * at + core, st) for at in plane_at]
+    st_at = [lax.rem(st + offset, n_st) for offset in range(n_st)]
+    ev_at = [lax.rem(ev + offset, n_ev) for offset in range(n_ev)]
+
+    barrier = pltpu.get_barrier_semaphore()
+    for offset in range(1, n_ev):
+        pl.semaphore_signal(barrier, inc=1, device_id=(ev_at[offset], st), device_id_type=MESH)
+    for offset in range(1, n_st):
+        pl.semaphore_signal(barrier, inc=1, device_id=(ev, st_at[offset]), device_id_type=MESH)
 
     loads = [
         pltpu.make_async_copy(src, dst, load_sem.at[index])
@@ -116,10 +121,6 @@
 
     for index in range(blocks):
         fetch(index).start()
-
-    barrier = pltpu.get_barrier_semaphore()
-    for offset in range(1, n_dev):
-        pl.semaphore_signal(barrier, inc=1, device_id=peer(offset), device_id_type=MESH)
 
     for load in loads:
         load.wait()
@@ -140,27 +141,81 @@
     mix[waves:, :starts] = (-coef_imag).astype(BF16)
     mix[waves:, starts:] = coef_real.astype(BF16)
     sums[...] = jnp.zeros_like(sums)
-    count_tell[0:1, :] = jnp.full((1, 128), limit, jnp.int32).astype(F32)
-
-    pl.semaphore_wait(barrier, n_dev - 1)
-
-    def count_copy(offset, slot):
+
+    def tiny_copy(kind, stage, dst, send, recv, to):
         return pltpu.make_async_remote_copy(
-            src_ref=count_tell.at[pl.ds(0, 1), :],
-            dst_ref=count_heard.at[slot, pl.ds(0, 1), :],
-            send_sem=count_send.at[offset],
-            recv_sem=count_recv.at[slot],
-            device_id=peer(offset),
+            src_ref=tiny.at[kind, stage],
+            dst_ref=dst,
+            send_sem=tiny_send.at[kind, send],
+            recv_sem=tiny_recv.at[kind, recv],
+            device_id=to,
             device_id_type=MESH,
         )
 
-    for offset in range(1, n_dev):
-        count_copy(offset, me).start()
-    count_heard[me, 0:1, :] = count_tell[0:1, :]
+    def tiny_core_copy(kind):
+        return tiny_copy(kind, 0, tiny_core.at[kind], 0, 0, partner)
+
+    def tiny_plane_copy(kind, offset, at):
+        return tiny_copy(kind, 1, tiny_plane.at[kind, at], offset, 1 + at, plane_to[offset])
+
+    def tiny_st_copy(kind, offset, at):
+        return tiny_copy(
+            kind,
+            2,
+            tiny_st.at[kind, at],
+            planes + offset,
+            1 + planes + at,
+            (ev, st_at[offset]),
+        )
+
+    def tiny_core_stage(kind, value):
+        tiny[kind, 0] = value
+        tiny_core_copy(kind).start()
+
+    def tiny_plane_stage(kind):
+        tiny_core_copy(kind).wait_recv()
+        value = tiny[kind, 0] + tiny_core[kind]
+        tiny[kind, 1] = value
+        for offset in range(1, planes):
+            tiny_plane_copy(kind, offset, plane).start()
+        tiny_plane[kind, plane] = value
+
+    def tiny_st_stage(kind):
+        for offset in range(1, planes):
+            tiny_plane_copy(kind, offset, plane_at[offset]).wait_recv()
+        value = tiny_plane[kind, 0]
+        for index in range(1, planes):
+            value = value + tiny_plane[kind, index]
+        tiny[kind, 2] = value
+        for offset in range(1, n_st):
+            tiny_st_copy(kind, offset, st).start()
+        tiny_st[kind, st] = value
+
+    def tiny_total(kind):
+        for offset in range(1, n_st):
+            tiny_st_copy(kind, offset, st_at[offset]).wait_recv()
+        value = tiny_st[kind, 0]
+        for index in range(1, n_st):
+            value = value + tiny_st[kind, index]
+        return value
 
     def block_step(step, carry):
         first = pl.multiple_of(step * BLOCK, BLOCK)
         fetch(step).wait()
+
+        @pl.when(step == 1)
+        def _():
+            pl.semaphore_wait(barrier, n_ev + n_st - 2)
+            tiny_core_stage(0, jnp.full((8, 128), limit, jnp.int32).astype(F32))
+
+        @pl.when(step == 2)
+        def _():
+            tiny_plane_stage(0)
+
+        @pl.when(step == 3)
+        def _():
+            tiny_st_stage(0)
+
         mass = mass_ref[step]
         mass2[...] = jnp.broadcast_to(mass * mass, (128, BLOCK)).T
 
@@ -200,32 +255,8 @@
 
     lax.fori_loop(0, blocks, block_step, 0)
 
-    lane = lax.broadcasted_iota(jnp.int32, (1, 128), 1)
-    for z in range(n_st):
-        log_row = pltpu.roll(sums[0:1, :], 128 - z * group, 1) if z else sums[0:1, :]
-        sim_row = pltpu.roll(sums[1:2, :], (128 + group - z * group) % 128, 1) if z != 1 else sums[1:2, :]
-        tell[z, 0:1, :] = jnp.where(lane < group, log_row, sim_row)
-
-    def tell_copy(offset, slot):
-        to_ev, to_st = peer(offset)
-        return pltpu.make_async_remote_copy(
-            src_ref=tell.at[to_st, pl.ds(0, 1), :],
-            dst_ref=heard.at[slot, pl.ds(0, 1), :],
-            send_sem=tell_send.at[offset],
-            recv_sem=tell_recv.at[slot],
-            device_id=(to_ev, to_st),
-            device_id_type=MESH,
-        )
-
-    for offset in range(1, n_dev):
-        tell_copy(offset, me).start()
-    heard[me, 0:1, :] = tell[st, 0:1, :]
-
-    for offset in range(1, n_dev):
-        count_copy(offset, lax.rem(me + offset, n_dev)).wait_recv()
-    n_data = count_heard[0, 0:1, :]
-    for index in range(1, n_dev):
-        n_data = n_data + count_heard[index, 0:1, :]
+    tiny_core_stage(1, sums[...])
+    n_data = tiny_total(0)[0:1, :]
     n_sim = events - n_data
     ratio = jnp.broadcast_to((n_sim / n_data)[:, 0:1], (2 * starts, BLOCK))
     final = jnp.broadcast_to((waves * scale / n_sim)[:, 0:1], (8, width))
@@ -249,23 +280,23 @@
             dst_ref=core_in.at[part],
             send_sem=core_send.at[part],
             recv_sem=core_recv.at[part],
-            device_id=(2 * plane + 1 - core, st),
+            device_id=partner,
             device_id_type=MESH,
         )
 
     def plane_copy(part, offset):
-        to = lax.rem(plane + offset, planes)
+        to = plane_at[offset]
         return pltpu.make_async_remote_copy(
             src_ref=plane_sum.at[part, to],
             dst_ref=plane_in.at[part, offset],
             send_sem=plane_send.at[part, offset],
             recv_sem=plane_recv.at[part, offset],
-            device_id=(2 * to + core, st),
+            device_id=plane_to[offset],
             device_id_type=MESH,
         )
 
     def st_copy(part, offset):
-        to = lax.rem(st + offset, n_st)
+        to = st_at[offset]
         return pltpu.make_async_remote_copy(
             src_ref=st_sum.at[part, to],
             dst_ref=st_in.at[part, offset],
@@ -281,11 +312,12 @@
             dst_ref=done_in.at[part, slot],
             send_sem=done_send.at[part, offset],
             recv_sem=done_recv.at[part, slot],
-            device_id=(lax.rem(ev + offset, n_ev), st),
+            device_id=(ev_at[offset], st),
             device_id_type=MESH,
         )
 
     slot = core * planes + plane
+    ev_slot = [lax.rem(at, 2) * planes + lax.div(at, 2) for at in ev_at]
 
     def make_part(part):
         real_cols = pl.ds(part * part_waves, part_waves)
@@ -337,18 +369,21 @@
             st_stage(tick - 2)
         if 0 <= tick - 1 < parts:
             plane_stage(tick - 1)
-
-    for offset in range(1, n_dev):
-        tell_copy(offset, lax.rem(me + offset, n_dev)).wait_recv()
-    total = heard[0, 0:1, :]
-    for index in range(1, n_dev):
-        total = total + heard[index, 0:1, :]
-    like_ref[...] = pltpu.roll(total, 128 - group, 1) / n_sim - total / n_data
+        if tick == 0:
+            tiny_plane_stage(1)
+        if tick == 1:
+            tiny_st_stage(1)
+
+    total = tiny_total(1)
+    like_all = total[1:2, :] / n_sim - total[0:1, :] / n_data
+    like = like_all
+    for z in range(1, n_st):
+        like = jnp.where(st == z, pltpu.roll(like_all, 128 - z * group, 1), like)
+    like_ref[...] = like
 
     for part in range(parts):
         for offset in range(1, n_ev):
-            other = lax.rem(ev + offset, n_ev)
-            done_copy(part, offset, lax.rem(other, 2) * planes + other // 2).wait_recv()
+            done_copy(part, offset, ev_slot[offset]).wait_recv()
         for index in range(n_ev):
             row, col = place(index)
             at = part * part_waves + col
@@ -356,9 +391,12 @@
                 at += waves - part_waves
             out_ref[row : row + 8, at : at + width] = done_in[part, index]
 
-    for offset in range(1, n_dev):
-        count_copy(offset, me).wait_send()
-        tell_copy(offset, me).wait_send()
+    for kind in range(2):
+        tiny_core_copy(kind).wait_send()
+        for offset in range(1, planes):
+            tiny_plane_copy(kind, offset, plane).wait_send()
+        for offset in range(1, n_st):
+            tiny_st_copy(kind, offset, st).wait_send()
     for part in range(parts):
         core_copy(part).wait_send()
         for offset in range(1, planes):
@@ -416,10 +454,10 @@
                 vmem((8, 128), F32),
                 vmem((blocks, 2 * starts, BLOCK), F32),
                 vmem((2 * starts, rows), BF16),
-                vmem((8, 128), F32),
-                vmem((n_dev, 8, 128), F32),
-                vmem((n_st, 8, 128), F32),
-                vmem((n_dev, 8, 128), F32),
+                vmem((2, 3, 8, 128), F32),
+                vmem((2, 8, 128), F32),
+                vmem((2, planes, 8, 128), F32),
+                vmem((2, n_st, 8, 128), F32),
                 vmem((parts, 2, planes, n_st, *piece), F32),
                 vmem((parts, planes, n_st, *piece), F32),
                 vmem((parts, planes, n_st, *piece), F32),
@@ -430,10 +468,8 @@
                 vmem((parts, n_ev, *piece), F32),
                 dma((7,)),
                 dma((blocks,)),
-                dma((n_dev,)),
-                dma((n_dev,)),
-                dma((n_dev,)),
-                dma((n_dev,)),
+                dma((2, planes + n_st)),
+                dma((2, 1 + planes + n_st)),
                 dma((parts,)),
                 dma((parts,)),
                 dma((parts, planes)),

time: 64.5 us -> 64.1 us (level)
  no operation moved by 1% of the time
where the time goes in v3:
time: 64.1 us; the launch traced here: 64 us
  Pallas kernels  59.9 us (93%)
  local copies, waits for them, and re-layouts  2.8 us (4%)
  between operations  1.29 us (2%)
    pallas_call x1, Pallas kernels, shards(): pl.pallas_call(functools.partial(fit_kernel, n_ev, n_st, parts), in_specs...  59.9 us
    unnamed x1, local copies, waits for them, and re-layouts  1.67 us

profile of v3, /device:TPU:0, one launch (start us, length us, event | category | flops | bytes accessed | tf_op | source)
XLA Modules:
  0.0 64.0 jit_solution(8403461959341578237)
XLA Ops:
  1.3 59.9 %fit_all.1 = (f32[32,2048]{1,0:T(8,128)}, f32[1,128]{1,0:T(1,128)}) custom-call(s32[1]{0:T(128)S(6)} %copy.11.limit_hbm, f32[32]{0:T(128)} %pole_mass_hbm.1, f32[32]{0:T(128)} %pole_width_hbm.1, bf16[4096,2048]{1,0:T(8,128)(2,1)} %amp_hbm.1, f32[8,1,512]{2,1,0:T(1,128)} %bitcast.5, s32[1,1024]{1,0:T(1,128)} %bitcast.6, f32[128,2048]{1,0:T(8,128)} %coef_hbm.1, ...), custom_call_target="tpu_custom_call" | custom-call | tf_op jit(solution)/shard_map/fit_all/pallas_call | solution.py:433
  61.2 1.1 %slice_bitcast_fusion = f32[32]{0:T(128)} fusion(f32[1,128]{1,0:T(1,128)} %get-tuple-element.5), kind=kLoop, calls=%fused_computation | loop fusion | bytes 256 | tf_op jit(solution)/shard_map/squeeze | solution.py:496
  62.3 1.7 %copy.12 = f32[32,2048]{1,0:T(8,128)} copy(f32[32,2048]{1,0:T(8,128)} %get-tuple-element.8) | data formatting | bytes 524288

commit v4 on v3

--- a/solution.py
+++ b/solution.py
@@ -239,7 +239,7 @@
                 amp_ref[here, imag_cols] = ((amp_imag * u + amp_real) * r).astype(BF16)
             return carry
 
-        lax.fori_loop(0, BLOCK // ROWS, dress, 0)
+        lax.fori_loop(0, BLOCK // ROWS, dress, 0, unroll=2)
 
         dressed = amp_ref[pl.ds(first, BLOCK), :]
         value = jnp.dot(dressed, mix[...], preferred_element_type=F32) * scale
@@ -360,19 +360,26 @@
             done_copy(part, offset, slot).start()
         done_in[part, slot] = total
 
-    for tick in range(parts + 3):
-        if tick < parts:
-            make_part(tick)
-        if 0 <= tick - 3 < parts:
-            done_stage(tick - 3)
-        if 0 <= tick - 2 < parts:
-            st_stage(tick - 2)
-        if 0 <= tick - 1 < parts:
-            plane_stage(tick - 1)
-        if tick == 0:
+    for part in range(parts):
+        make_part(part)
+        if part >= 1:
+            plane_stage(part - 1)
+        if part >= 3:
+            st_stage(part - 3)
+        if part == 0:
             tiny_plane_stage(1)
-        if tick == 1:
+        if part == 1:
             tiny_st_stage(1)
+    if parts >= 3:
+        st_stage(parts - 3)
+    plane_stage(parts - 1)
+    for part in range(max(parts - 2, 0)):
+        done_stage(part)
+    if parts >= 2:
+        st_stage(parts - 2)
+    st_stage(parts - 1)
+    for part in range(max(parts - 2, 0), parts):
+        done_stage(part)
 
     total = tiny_total(1)
     like_all = total[1:2, :] / n_sim - total[0:1, :] / n_data
@@ -480,7 +487,7 @@
                 dma((parts, n_ev)),
             ],
             compiler_params=pltpu.CompilerParams(
-                collective_id=0, has_side_effects=True, vmem_limit_bytes=56 * 1024 * 1024
+                collective_id=0, has_side_effects=True, vmem_limit_bytes=40 * 1024 * 1024
             ),
             name="fit_all",
         )(

time: 64.1 us -> 56.4 us (0.88)
  Pallas kernels: 59.9 us -> 49 us
  local copies, waits for them, and re-layouts: 2.8 us -> 5.8 us
    pallas_call x1, Pallas kernels: 59.9 us -> 49 us  [shards(): pl.pallas_call(functools.partial(fit_kernel, n_ev, n_st, parts), in_specs...]
    unnamed x1 -> x13, local copies, waits for them, and re-layouts: 1.67 us -> 5.29 us
where the time goes in v4:
time: 56.4 us; the launch traced here: 56.1 us
  Pallas kernels  49 us (87%)
  local copies, waits for them, and re-layouts  5.8 us (10%)
  between operations  1.3 us (2%)
    pallas_call x1, Pallas kernels, shards(): pl.pallas_call(functools.partial(fit_kernel, n_ev, n_st, parts), in_specs...  49 us
    unnamed x13, local copies, waits for them, and re-layouts  5.29 us

profile of v4, /device:TPU:0, one launch (start us, length us, event | category | flops | bytes accessed | tf_op | source)
XLA Modules:
  0.0 56.1 jit_solution(1013145798649366319)
XLA Ops:
  1.3 0.0 copy-start
  1.3 1.2 %copy-done = f32[128,2048]{1,0:T(8,128)S(1)} copy-done((f32[128,2048]{1,0:T(8,128)S(1)}, f32[128,2048]{1,0:T(8,128)}, u32[]{:S(2)}) %copy-start) | copy-done | bytes 1048600
  2.5 0.0 copy-start.1
  2.5 0.7 %copy-done.1 = f32[4096]{0:T(1024)S(1)} copy-done((f32[4096]{0:T(1024)S(1)}, f32[4096]{0:T(1024)}, u32[]{:S(2)}) %copy-start.1) | copy-done | bytes 16408
  3.2 0.0 copy-start.2
  3.2 0.7 %copy-done.2 = s32[1024]{0:T(1024)S(1)} copy-done((s32[1024]{0:T(1024)S(1)}, s32[1024]{0:T(1024)}, u32[]{:S(2)}) %copy-start.2) | copy-done | bytes 4120
  3.9 0.0 copy-start.3
  3.9 0.7 %copy-done.3 = f32[32]{0:T(128)S(1)} copy-done((f32[32]{0:T(128)S(1)}, f32[32]{0:T(128)}, u32[]{:S(2)}) %copy-start.3) | copy-done | bytes 152
  4.6 0.0 copy-start.4
  4.6 0.7 %copy-done.4 = f32[32]{0:T(128)S(1)} copy-done((f32[32]{0:T(128)S(1)}, f32[32]{0:T(128)}, u32[]{:S(2)}) %copy-start.4) | copy-done | bytes 152
  5.2 0.0 copy-start.5
  5.2 0.7 %copy-done.5 = f32[128]{0:T(128)S(1)} copy-done((f32[128]{0:T(128)S(1)}, f32[128]{0:T(128)}, u32[]{:S(2)}) %copy-start.5) | copy-done | bytes 536
  5.9 49.0 %fit_all.1 = (f32[32,2048]{1,0:T(8,128)S(1)}, f32[1,128]{1,0:T(1,128)S(1)}) custom-call(s32[1]{0:T(128)S(6)} %copy.11.limit_hbm, f32[32]{0:T(128)S(1)} %copy-done.3, f32[32]{0:T(128)S(1)} %copy-done.4, bf16[4096,2048]{1,0:T(8,128)(2,1)} %amp_hbm.1, f32[8,1,512]{2,1,0:T(1,128)S(1)} %bitcast.5, s32[1,1024]{1,0:T(1,128)S(1)} %bitcast.6, ...), custom_call_target="tpu_custom_call" | custom-call | tf_op jit(solution)/shard_map/fit_all/pallas_call | solution.py:440
  54.9 0.5 slice_bitcast_fusion
  55.4 0.7 %copy.12 = f32[32,2048]{1,0:T(8,128)} copy(f32[32,2048]{1,0:T(8,128)S(1)} %get-tuple-element.8) | data formatting | bytes 524288
Async XLA Ops:
  1.3 1.2 %copy-start = (f32[128,2048]{1,0:T(8,128)S(1)}, f32[128,2048]{1,0:T(8,128)}, u32[]{:S(2)}) copy-start(f32[128,2048]{1,0:T(8,128)} %coef_hbm.1) | copy-start | bytes 3145732
  2.5 0.7 %copy-start.1 = (f32[4096]{0:T(1024)S(1)}, f32[4096]{0:T(1024)}, u32[]{:S(2)}) copy-start(f32[4096]{0:T(1024)} %param.9) | copy-start | bytes 49156
  3.2 0.7 %copy-start.2 = (s32[1024]{0:T(1024)S(1)}, s32[1024]{0:T(1024)}, u32[]{:S(2)}) copy-start(s32[1024]{0:T(1024)} %param.11) | copy-start | bytes 12292
  3.9 0.7 %copy-start.3 = (f32[32]{0:T(128)S(1)}, f32[32]{0:T(128)}, u32[]{:S(2)}) copy-start(f32[32]{0:T(128)} %pole_mass_hbm.1) | copy-start | bytes 388
  4.6 0.7 %copy-start.4 = (f32[32]{0:T(128)S(1)}, f32[32]{0:T(128)}, u32[]{:S(2)}) copy-start(f32[32]{0:T(128)} %pole_width_hbm.1) | copy-start | bytes 388
  5.2 0.7 %copy-start.5 = (f32[128]{0:T(128)S(1)}, f32[128]{0:T(128)}, u32[]{:S(2)}) copy-start(f32[128]{0:T(128)} %param.15) | copy-start | bytes 1540

commit v5 on v4

--- a/solution.py
+++ b/solution.py
@@ -239,7 +239,7 @@
                 amp_ref[here, imag_cols] = ((amp_imag * u + amp_real) * r).astype(BF16)
             return carry
 
-        lax.fori_loop(0, BLOCK // ROWS, dress, 0, unroll=2)
+        lax.fori_loop(0, BLOCK // ROWS, dress, 0, unroll=4)
 
         dressed = amp_ref[pl.ds(first, BLOCK), :]
         value = jnp.dot(dressed, mix[...], preferred_element_type=F32) * scale

time: 56.4 us -> 56 us (level)
  no operation moved by 1% of the time
where the time goes in v5:
time: 56 us; the launch traced here: 55.7 us
  Pallas kernels  48.6 us (87%)
  local copies, waits for them, and re-layouts  5.8 us (10%)
  between operations  1.3 us (2%)
    pallas_call x1, Pallas kernels, shards(): pl.pallas_call(functools.partial(fit_kernel, n_ev, n_st, parts), in_specs...  48.6 us
    unnamed x13, local copies, waits for them, and re-layouts  5.29 us

profile of v5, /device:TPU:0, one launch (start us, length us, event | category | flops | bytes accessed | tf_op | source)
XLA Modules:
  0.0 55.7 jit_solution(139397097113113119)
XLA Ops:
  1.3 0.0 copy-start
  1.3 1.2 %copy-done = f32[128,2048]{1,0:T(8,128)S(1)} copy-done((f32[128,2048]{1,0:T(8,128)S(1)}, f32[128,2048]{1,0:T(8,128)}, u32[]{:S(2)}) %copy-start) | copy-done | bytes 1048600
  2.5 0.0 copy-start.1
  2.5 0.7 %copy-done.1 = f32[4096]{0:T(1024)S(1)} copy-done((f32[4096]{0:T(1024)S(1)}, f32[4096]{0:T(1024)}, u32[]{:S(2)}) %copy-start.1) | copy-done | bytes 16408
  3.2 0.0 copy-start.2
  3.2 0.7 %copy-done.2 = s32[1024]{0:T(1024)S(1)} copy-done((s32[1024]{0:T(1024)S(1)}, s32[1024]{0:T(1024)}, u32[]{:S(2)}) %copy-start.2) | copy-done | bytes 4120
  3.9 0.0 copy-start.3
  3.9 0.7 %copy-done.3 = f32[32]{0:T(128)S(1)} copy-done((f32[32]{0:T(128)S(1)}, f32[32]{0:T(128)}, u32[]{:S(2)}) %copy-start.3) | copy-done | bytes 152
  4.6 0.0 copy-start.4
  4.6 0.7 %copy-done.4 = f32[32]{0:T(128)S(1)} copy-done((f32[32]{0:T(128)S(1)}, f32[32]{0:T(128)}, u32[]{:S(2)}) %copy-start.4) | copy-done | bytes 152
  5.2 0.0 copy-start.5
  5.2 0.7 %copy-done.5 = f32[128]{0:T(128)S(1)} copy-done((f32[128]{0:T(128)S(1)}, f32[128]{0:T(128)}, u32[]{:S(2)}) %copy-start.5) | copy-done | bytes 536
  5.9 48.6 %fit_all.1 = (f32[32,2048]{1,0:T(8,128)S(1)}, f32[1,128]{1,0:T(1,128)S(1)}) custom-call(s32[1]{0:T(128)S(6)} %copy.11.limit_hbm, f32[32]{0:T(128)S(1)} %copy-done.3, f32[32]{0:T(128)S(1)} %copy-done.4, bf16[4096,2048]{1,0:T(8,128)(2,1)} %amp_hbm.1, f32[8,1,512]{2,1,0:T(1,128)S(1)} %bitcast.5, s32[1,1024]{1,0:T(1,128)S(1)} %bitcast.6, ...), custom_call_target="tpu_custom_call" | custom-call | tf_op jit(solution)/shard_map/fit_all/pallas_call | solution.py:440
  54.4 0.5 slice_bitcast_fusion
  54.9 0.7 %copy.12 = f32[32,2048]{1,0:T(8,128)} copy(f32[32,2048]{1,0:T(8,128)S(1)} %get-tuple-element.8) | data formatting | bytes 524288
Async XLA Ops:
  1.3 1.2 %copy-start = (f32[128,2048]{1,0:T(8,128)S(1)}, f32[128,2048]{1,0:T(8,128)}, u32[]{:S(2)}) copy-start(f32[128,2048]{1,0:T(8,128)} %coef_hbm.1) | copy-start | bytes 3145732
  2.5 0.7 %copy-start.1 = (f32[4096]{0:T(1024)S(1)}, f32[4096]{0:T(1024)}, u32[]{:S(2)}) copy-start(f32[4096]{0:T(1024)} %param.9) | copy-start | bytes 49156
  3.2 0.7 %copy-start.2 = (s32[1024]{0:T(1024)S(1)}, s32[1024]{0:T(1024)}, u32[]{:S(2)}) copy-start(s32[1024]{0:T(1024)} %param.11) | copy-start | bytes 12292
  3.9 0.7 %copy-start.3 = (f32[32]{0:T(128)S(1)}, f32[32]{0:T(128)}, u32[]{:S(2)}) copy-start(f32[32]{0:T(128)} %pole_mass_hbm.1) | copy-start | bytes 388
  4.6 0.7 %copy-start.4 = (f32[32]{0:T(128)S(1)}, f32[32]{0:T(128)}, u32[]{:S(2)}) copy-start(f32[32]{0:T(128)} %pole_width_hbm.1) | copy-start | bytes 388
  5.2 0.7 %copy-start.5 = (f32[128]{0:T(128)S(1)}, f32[128]{0:T(128)}, u32[]{:S(2)}) copy-start(f32[128]{0:T(128)} %param.15) | copy-start | bytes 1540
